TPU v7x, 32 devices: a whole 2x2x4 slice. The times are simulated.
32 devices in a mesh: dp: 4 (over y, core), row: 2 (over x), col: 4 (over z).
Axes of the slice: x: 2, y: 2, z: 4, core: 2. Of those that a mesh axis runs over, the one named last changes fastest.
Arguments:
- inputs: bfloat16 [4096, 2048], P(('dp', 'col'), 'row'), may hold values from -6 to 6
- first_gain: float32 [1, 2048], P(None, 'row'), may hold values from 0.25 to 1.75
- first_shift: float32 [1, 2048], P(None, 'row'), may hold values from -3 to 3
- project_in: bfloat16 [1, 2048, 3, 2048], P(None, 'row', None, 'col'), may hold values from -0.125 to 0.125
- project_bias: float32 [1, 3, 2048], P(None, None, 'col'), may hold values from -3 to 3
- project_out: bfloat16 [1, 2048, 2048], P(None, 'col', 'row'), may hold values from -0.75 to 0.75
- second_gain: float32 [1, 2048], P(None, 'row'), may hold values from 0.25 to 1.75
- second_shift: float32 [1, 2048], P(None, 'row'), may hold values from -3 to 3
- gate_weight: bfloat16 [1, 2048, 2, 5632], P(None, 'row', None, 'col'), may hold values from -0.125 to 0.125
- down_weight: bfloat16 [1, 5632, 2048], P(None, 'col', 'row'), may hold values from -0.078125 to 0.078125
- cotangent: bfloat16 [4096, 2048], P(('dp', 'col'), 'row'), may hold values from -6 to 6
Outputs:
- layer_outputs: bfloat16 [1, 4096, 2048], P(None, ('dp', 'col'), 'row')
- input_grad: float32 [4096, 2048], P(('dp', 'col'), 'row')
- first_gain_grad: float32 [1, 2048], P(None, 'row')
- first_shift_grad: float32 [1, 2048], P(None, 'row')
- project_in_grad: float32 [1, 2048, 3, 2048], P(None, 'row', None, 'col')
- project_bias_grad: float32 [1, 3, 2048], P(None, None, 'col')
- project_out_grad: float32 [1, 2048, 2048], P(None, 'col', 'row')
- second_gain_grad: float32 [1, 2048], P(None, 'row')
- second_shift_grad: float32 [1, 2048], P(None, 'row')
- gate_weight_grad: float32 [1, 2048, 2, 5632], P(None, 'row', None, 'col')
- down_weight_grad: float32 [1, 5632, 2048], P(None, 'col', 'row')
All inputs are finite; a program needn't handle non-finite values.
Results may differ from a plain program's by a relative error of at most 0.015.
Values may be sent and summed in bfloat16 or wider, within the bound.
No kernel may reach another device: no remote copies, remote signals or barrier semaphores. Data moves between devices by JAX's collectives and lax.ppermute only.
A program may use at most 192 MiB of HBM per device.

v0:
```python
import math
import jax
import jax.numpy as jnp
from jax import lax
from jax.sharding import PartitionSpec as P

HEAD_DIM = 64
ROT = 16
LENGTH = 1024
EPSILON = 1e-05


def rotary_tables(tokens):
    position = (jnp.arange(tokens) % LENGTH).astype(jnp.float32)
    frequency = 10000.0 ** (-(jnp.arange(ROT // 2).astype(jnp.float32) * 2.0 / ROT))
    angles = position[:, None] * frequency[None, :]
    return (jnp.cos(angles), jnp.sin(angles))


def rotate(tensor, cosine_table, sine_table):
    half_rot = ROT // 2
    front_half = tensor[..., :half_rot]
    back_half = tensor[..., half_rot:ROT]
    cosine = cosine_table[:, None, :]
    sine = sine_table[:, None, :]
    return jnp.concatenate(
        [
            front_half * cosine - back_half * sine,
            back_half * cosine + front_half * sine,
            tensor[..., ROT:],
        ],
        axis=-1,
    )


def row_totals(first_part, second_part):
    return lax.psum((first_part, second_part), "row")


def norm_forward(stream, gain_row, shift_row):
    features = stream.shape[1] * lax.axis_size("row")
    summed, squares = row_totals(jnp.sum(stream, axis=1), jnp.sum(stream * stream, axis=1))
    average = summed / features
    variance = squares / features - average * average
    inv_root = lax.rsqrt(variance + EPSILON)
    normed = (stream - average[:, None]) * inv_root[:, None]
    return (normed, inv_root, (normed * gain_row + shift_row).astype(jnp.bfloat16))


def norm_backward(gradient, normed, inv_root, gain_row):
    features = gradient.shape[1] * lax.axis_size("row")
    scaled = gradient * gain_row
    summed, crossed = row_totals(jnp.sum(scaled, axis=1), jnp.sum(scaled * normed, axis=1))
    stream_grad = inv_root[:, None] * (
        scaled - summed[:, None] / features - normed * crossed[:, None] / features
    )
    return (stream_grad, jnp.sum(gradient * normed, axis=0), jnp.sum(gradient, axis=0))


def gather_tokens(local_low):
    return lax.all_gather(local_low, "col", axis=0, tiled=True)


def gather_gradient(local_low):
    return lax.all_gather(local_low, "col", axis=0, tiled=True)


def split_units(partial_sum):
    return lax.psum_scatter(partial_sum, "row", scatter_dimension=2, tiled=True)


def join_units(local_units):
    return lax.all_gather(local_units, "row", axis=1, tiled=True)


def split_unit_grads(partial_sum):
    return lax.psum_scatter(partial_sum, "row", scatter_dimension=1, tiled=True)


def join_unit_grads(local_units):
    return lax.all_gather(local_units, "row", axis=2, tiled=True)


def branch_sum(full_rows, weight_block):
    return lax.psum_scatter(
        jnp.dot(full_rows, weight_block, preferred_element_type=jnp.float32),
        "col",
        scatter_dimension=0,
        tiled=True,
    )


def input_sum(grad_full, weight_block):
    return lax.psum_scatter(
        jnp.einsum("stk,dtk->sd", grad_full, weight_block, preferred_element_type=jnp.float32),
        "col",
        scatter_dimension=0,
        tiled=True,
    )


def weight_product(normed, gain_row, shift_row, grad_full):
    local_low = (normed * gain_row + shift_row).astype(jnp.bfloat16)
    return jnp.einsum(
        "sd,stk->dtk",
        lax.all_gather(local_low, "col", axis=0, tiled=True),
        grad_full,
        preferred_element_type=jnp.float32,
    )


def block_scores(query_heads, key_heads, value_heads, block_index, factor):
    block_rows = min(512, LENGTH)
    offset = block_index * block_rows
    seq_begin = offset // LENGTH * LENGTH
    query_block = lax.dynamic_slice_in_dim(query_heads, offset, block_rows, 0)
    scores = (
        jnp.einsum("qhd,khd->hqk", query_block, key_heads, preferred_element_type=jnp.float32)
        * factor
    )
    query_position = offset - seq_begin + jnp.arange(block_rows)
    causal = query_position[:, None] >= jnp.arange(LENGTH)[None, :]
    scores = jnp.where(causal[None], scores, -jnp.inf)
    return (scores, query_block, key_heads, value_heads, offset, seq_begin)


def attend_forward(query_heads, key_heads, value_heads, factor):
    tokens = query_heads.shape[0]
    block_rows = min(512, LENGTH)

    def one_block(block_index):
        scores, query_block, key_block, value_block, offset, seq_begin = block_scores(
            query_heads, key_heads, value_heads, block_index, factor
        )
        highest = jnp.max(scores, axis=-1, keepdims=True)
        exponent = jnp.exp(scores - highest)
        summed = jnp.sum(exponent, axis=-1, keepdims=True)
        softmax_low = (exponent / summed).astype(jnp.bfloat16)
        attended = jnp.einsum(
            "hqk,khd->qhd", softmax_low, value_block, preferred_element_type=jnp.float32
        )
        return (attended, (highest + jnp.log(summed))[..., 0])

    attended, log_total = lax.map(one_block, jnp.arange(tokens // block_rows))
    return (attended.reshape(tokens, -1), log_total)


def attend_backward(query_heads, key_heads, value_heads, out_heads, log_total, factor):
    tokens = query_heads.shape[0]
    block_rows = min(512, LENGTH)

    def one_block(carry, block_index):
        key_grad, value_grad = carry
        scores, query_block, key_block, value_block, offset, seq_begin = block_scores(
            query_heads, key_heads, value_heads, block_index, factor
        )
        softmax_probs = jnp.exp(scores - log_total[block_index][..., None])
        grad_block = lax.dynamic_slice_in_dim(out_heads, offset, block_rows, 0)
        prob_grad = jnp.einsum(
            "qhd,khd->hqk", grad_block, value_block, preferred_element_type=jnp.float32
        )
        shift_term = jnp.sum(softmax_probs * prob_grad, axis=-1, keepdims=True)
        score_grad = (softmax_probs * (prob_grad - shift_term)).astype(jnp.bfloat16)
        query_grad = (
            jnp.einsum("hqk,khd->qhd", score_grad, key_block, preferred_element_type=jnp.float32)
            * factor
        )
        key_part = (
            jnp.einsum("hqk,qhd->khd", score_grad, query_block, preferred_element_type=jnp.float32)
            * factor
        )
        value_part = jnp.einsum(
            "hqk,qhd->khd",
            softmax_probs.astype(jnp.bfloat16),
            grad_block,
            preferred_element_type=jnp.float32,
        )
        key_grad = key_grad + key_part
        value_grad = value_grad + value_part
        return ((key_grad, value_grad), query_grad)

    zeros_start = jnp.zeros(key_heads.shape, jnp.float32)
    (key_grad, value_grad), query_grad = lax.scan(
        one_block, (zeros_start, zeros_start), jnp.arange(tokens // block_rows)
    )
    return (query_grad.reshape(key_heads.shape), key_grad, value_grad)


def local(
    inputs,
    first_gain,
    first_shift,
    project_in,
    project_bias,
    project_out,
    second_gain,
    second_shift,
    gate_weight,
    down_weight,
    cotangent,
):
    layers = project_in.shape[0]
    tokens = inputs.shape[0] * lax.axis_size("col")
    heads_here = project_in.shape[3] // lax.axis_size("row") // HEAD_DIM
    bias_width = project_bias.shape[2] // lax.axis_size("row")
    row_place = lax.axis_index("row")
    factor = 1.0 / math.sqrt(HEAD_DIM)
    cosine_table, sine_table = rotary_tables(tokens)
    stream = inputs.astype(jnp.float32)
    layer_index = 0
    normed_a, inv_root_a, low_a = norm_forward(
        stream, first_gain[layer_index], first_shift[layer_index]
    )
    full_a = gather_tokens(low_a)
    partial_mix = jnp.einsum(
        "sd,dtk->stk", full_a, project_in[layer_index], preferred_element_type=jnp.float32
    )
    bias_here = lax.dynamic_slice_in_dim(
        project_bias[layer_index], row_place * bias_width, bias_width, 1
    )
    mixed = (split_units(partial_mix) + bias_here[None]).reshape(tokens, 3, heads_here, HEAD_DIM)
    query_heads = rotate(mixed[:, 0], cosine_table, sine_table).astype(jnp.bfloat16)
    key_heads = rotate(mixed[:, 1], cosine_table, sine_table).astype(jnp.bfloat16)
    value_heads = mixed[:, 2].astype(jnp.bfloat16)
    attended, log_total = attend_forward(query_heads, key_heads, value_heads, factor)
    heads_full = join_units(attended.astype(jnp.bfloat16))
    residual = stream + branch_sum(heads_full, project_out[layer_index])
    normed_b, inv_root_b, low_b = norm_forward(
        residual, second_gain[layer_index], second_shift[layer_index]
    )
    full_b = gather_tokens(low_b)
    gate_up = split_units(
        jnp.einsum(
            "sd,dtf->stf", full_b, gate_weight[layer_index], preferred_element_type=jnp.float32
        )
    )
    hidden = (jax.nn.silu(gate_up[:, 0]) * gate_up[:, 1]).astype(jnp.bfloat16)
    hidden_full = join_units(hidden)
    layer_out = (residual + branch_sum(hidden_full, down_weight[layer_index])).astype(jnp.bfloat16)
    outputs = [layer_out]
    kept_a = None
    kept_b = None
    saved = [
        (
            normed_a,
            inv_root_a,
            kept_a,
            query_heads,
            key_heads,
            value_heads,
            log_total,
            heads_full,
            normed_b,
            inv_root_b,
            kept_b,
            gate_up,
            hidden_full,
        )
    ]
    gradient = cotangent.astype(jnp.float32)
    in_grads = [None] * layers
    bias_grads = [None] * layers
    out_grads = [None] * layers
    gate_grads = [None] * layers
    down_grads = [None] * layers
    gain_a_grads = [None] * layers
    shift_a_grads = [None] * layers
    gain_b_grads = [None] * layers
    shift_b_grads = [None] * layers
    for layer_index in reversed(range(layers)):
        (
            normed_a,
            inv_root_a,
            kept_a,
            query_heads,
            key_heads,
            value_heads,
            log_total,
            heads_full,
            normed_b,
            inv_root_b,
            kept_b,
            gate_up,
            hidden_full,
        ) = saved[layer_index]
        grad_full = gather_gradient(gradient.astype(jnp.bfloat16))
        down_grad = jnp.einsum(
            "sf,sd->fd", hidden_full, grad_full, preferred_element_type=jnp.float32
        )
        hidden_grad = split_unit_grads(
            jnp.einsum(
                "sd,fd->sf", grad_full, down_weight[layer_index], preferred_element_type=jnp.float32
            )
        )
        gate_value = gate_up[:, 0]
        up_value = gate_up[:, 1]
        sigmoid_gate = jax.nn.sigmoid(gate_value)
        gate_grad = (
            hidden_grad * up_value * sigmoid_gate * (1.0 + gate_value * (1.0 - sigmoid_gate))
        )
        up_grad = hidden_grad * gate_value * sigmoid_gate
        gate_up_grad = jnp.stack([gate_grad, up_grad], axis=1).astype(jnp.bfloat16)
        gate_up_full = join_unit_grads(gate_up_grad)
        gate_weight_grad = weight_product(
            normed_b, second_gain[layer_index], second_shift[layer_index], gate_up_full
        )
        normed_b_grad = input_sum(gate_up_full, gate_weight[layer_index])
        back_b, gain_b_grad, shift_b_grad = norm_backward(
            normed_b_grad, normed_b, inv_root_b, second_gain[layer_index]
        )
        gradient_two = gradient + back_b
        grad_two_full = gather_gradient(gradient_two.astype(jnp.bfloat16))
        out_grad_weight = jnp.einsum(
            "sk,sd->kd", heads_full, grad_two_full, preferred_element_type=jnp.float32
        )
        attended_grad = split_unit_grads(
            jnp.einsum(
                "sd,kd->sk",
                grad_two_full,
                project_out[layer_index],
                preferred_element_type=jnp.float32,
            )
        )
        attended_grad = attended_grad.astype(jnp.bfloat16).reshape(tokens, heads_here, HEAD_DIM)
        query_grad, key_grad, value_grad = attend_backward(
            query_heads, key_heads, value_heads, attended_grad, log_total, factor
        )
        query_grad = rotate(query_grad, cosine_table, -sine_table)
        key_grad = rotate(key_grad, cosine_table, -sine_table)
        mixed_grad = (
            jnp.stack([query_grad, key_grad, value_grad], axis=1)
            .reshape(tokens, 3, heads_here * HEAD_DIM)
            .astype(jnp.bfloat16)
        )
        mixed_full = join_unit_grads(mixed_grad)
        bias_grad = jnp.sum(mixed_full, axis=0, dtype=jnp.float32)
        in_grad = weight_product(
            normed_a, first_gain[layer_index], first_shift[layer_index], mixed_full
        )
        normed_a_grad = input_sum(mixed_full, project_in[layer_index])
        back_a, gain_a_grad, shift_a_grad = norm_backward(
            normed_a_grad, normed_a, inv_root_a, first_gain[layer_index]
        )
        gradient = gradient_two + back_a
        in_grads[layer_index] = in_grad
        bias_grads[layer_index] = bias_grad
        out_grads[layer_index] = out_grad_weight
        gate_grads[layer_index] = gate_weight_grad
        down_grads[layer_index] = down_grad
        gain_a_grads[layer_index] = gain_a_grad
        shift_a_grads[layer_index] = shift_a_grad
        gain_b_grads[layer_index] = gain_b_grad
        shift_b_grads[layer_index] = shift_b_grad
    stack_in = jnp.stack(in_grads)
    stack_bias = jnp.stack(bias_grads)
    stack_out = jnp.stack(out_grads)
    stack_gate = jnp.stack(gate_grads)
    stack_down = jnp.stack(down_grads)
    stack_in, stack_bias, stack_out, stack_gate, stack_down = (
        lax.psum(stack_in.astype(jnp.bfloat16), "dp").astype(jnp.float32),
        lax.psum(stack_bias.astype(jnp.bfloat16), "dp").astype(jnp.float32),
        lax.psum(stack_out.astype(jnp.bfloat16), "dp").astype(jnp.float32),
        lax.psum(stack_gate.astype(jnp.bfloat16), "dp").astype(jnp.float32),
        lax.psum(stack_down.astype(jnp.bfloat16), "dp").astype(jnp.float32),
    )
    gain_a_total, shift_a_total, gain_b_total, shift_b_total = lax.psum(
        (
            jnp.stack(gain_a_grads),
            jnp.stack(shift_a_grads),
            jnp.stack(gain_b_grads),
            jnp.stack(shift_b_grads),
        ),
        ("dp", "col"),
    )
    return (
        jnp.stack(outputs),
        gradient,
        gain_a_total,
        shift_a_total,
        stack_in,
        stack_bias,
        stack_out,
        gain_b_total,
        shift_b_total,
        stack_gate,
        stack_down,
    )


def solution(mesh):
    return jax.shard_map(
        local,
        mesh=mesh,
        in_specs=(
            P(("dp", "col"), "row"),
            P(None, "row"),
            P(None, "row"),
            P(None, "row", None, "col"),
            P(None, None, "col"),
            P(None, "col", "row"),
            P(None, "row"),
            P(None, "row"),
            P(None, "row", None, "col"),
            P(None, "col", "row"),
            P(("dp", "col"), "row"),
        ),
        out_specs=(
            P(None, ("dp", "col"), "row"),
            P(("dp", "col"), "row"),
            P(None, "row"),
            P(None, "row"),
            P(None, "row", None, "col"),
            P(None, None, "col"),
            P(None, "col", "row"),
            P(None, "row"),
            P(None, "row"),
            P(None, "row", None, "col"),
            P(None, "col", "row"),
        ),
        check_vma=False,
    )
```

profile of v0, /device:TPU:0, one launch (start us, length us, event | category | flops | bytes accessed | tf_op | source)
XLA Modules:
  0.0 1484.0 jit_solution(7739865274060016093)
XLA Ops:
  17.3 47.9 %all-gather.9.cloned.1.call-done = bf16[1024,1024]{1,0:T(8,128)(2,1)} async-done(((bf16[256,1024]{1,0:T(8,128)(2,1)}), bf16[1024,1024]{1,0:T(8,128)(2,1)}) %all-gather.9.cloned.1.call-update) | async-done | bytes 2097168 | tf_op jit(solution)/shard_map/all_gather | solution.py:61
  73.6 74.4 %reduce-scatter.9.cloned.1.call-done = f32[1024,3,256]{2,0,1:T(8,128)} async-done(((f32[1024,3,512]{2,0,1:T(8,128)}), f32[1024,3,256]{2,0,1:T(8,128)}) %reduce-scatter.9.cloned.1.call-update) | async-done | bytes 3145744 | tf_op jit(solution)/shard_map/reduce_scatter | solution.py:69
  160.4 21.1 %while.31 = (s32[]{:T(128)}, bf16[2,512,4,64]{1,3,2,0:T(8,128)(2,1)}, f32[2,4,512]{2,1,0:T(4,128)S(1)}, s32[2]{0:T(128)S(1)}, bf16[1024,4,64]{0,2,1:T(8,128)(2,1...) while((s32[]{:T(128)}, ...), condition=%wide.region_8.9_spmd, body=%wide.region_5.8_spmd.sunk | while | flops 562559488 | bytes 35459536 | solution.py:144
  184.1 21.4 %all-gather.11.cloned.1.call-done = bf16[1024,512]{0,1:T(8,128)(2,1)} async-done(((bf16[1024,256]{0,1:T(8,128)(2,1)}), bf16[1024,512]{0,1:T(8,128)(2,1)}) %all-gather.11.cloned.1.call-update) | async-done | bytes 1048592 | tf_op jit(solution)/shard_map/all_gather | solution.py:73
  211.0 76.3 %reduce-scatter.11.cloned.1.call-done = f32[256,1024]{1,0:T(8,128)} async-done(((f32[1024,1024]{1,0:T(8,128)}), f32[256,1024]{1,0:T(8,128)}) %reduce-scatter.11.cloned.1.call-update) | async-done | bytes 1048592 | tf_op jit(solution)/shard_map/reduce_scatter | solution.py:85
  297.3 37.9 %all-gather.17.cloned.1.call-done = bf16[1024,1024]{1,0:T(8,128)(2,1)} async-done(((bf16[256,1024]{1,0:T(8,128)(2,1)}), bf16[1024,1024]{1,0:T(8,128)(2,1)}) %all-gather.17.cloned.1.call-update) | async-done | bytes 2097168 | tf_op jit(solution)/shard_map/all_gather | solution.py:65
  335.2 8.2 fusion.44
  343.5 38.4 %all-gather.13.cloned.1.call-done = bf16[1024,1024]{1,0:T(8,128)(2,1)} async-done(((bf16[256,1024]{1,0:T(8,128)(2,1)}), bf16[1024,1024]{1,0:T(8,128)(2,1)}) %all-gather.13.cloned.1.call-update) | async-done | bytes 2097168 | tf_op jit(solution)/shard_map/all_gather | solution.py:61
  381.9 11.9 fusion.35
  393.9 61.0 %reduce-scatter.17.cloned.1.call-done = f32[1024,704]{0,1:T(8,128)} async-done(((f32[1024,1408]{0,1:T(8,128)}), f32[1024,704]{0,1:T(8,128)}) %reduce-scatter.17.cloned.1.call-update) | async-done | bytes 2883600 | tf_op jit(solution)/shard_map/reduce_scatter | solution.py:77
  454.9 136.2 %reduce-scatter.13.cloned.1.call-done = f32[1024,2,704]{0,2,1:T(8,128)} async-done(((f32[1024,2,1408]{0,2,1:T(8,128)}), f32[1024,2,704]{0,2,1:T(8,128)}) %reduce-scatter.13.cloned.1.call-update) | async-done | bytes 5767184 | tf_op jit(solution)/shard_map/reduce_scatter | solution.py:69
  598.9 74.0 %all-gather.19.cloned.1.call-done = bf16[1024,2,1408]{0,2,1:T(8,128)(2,1)} async-done(((bf16[1024,2,704]{0,2,1:T(8,128)(2,1)}), bf16[1024,2,1408]{0,2,1:T(8,128)(2,1)}) %all-gather.19.cloned.1.call-update) | async-done | bytes 5767184 | tf_op jit(solution)/shard_map/all_gather | solution.py:81
  672.9 11.5 fusion.51
  684.4 32.5 %all-gather.15.cloned.1.call-done = bf16[1024,1408]{0,1:T(8,128)(2,1)} async-done(((bf16[1024,704]{0,1:T(8,128)(2,1)}), bf16[1024,1408]{0,1:T(8,128)(2,1)}) %all-gather.15.cloned.1.call-update) | async-done | bytes 2883600 | tf_op jit(solution)/shard_map/all_gather | solution.py:73
  716.9 8.2 fusion.46
  725.2 71.5 %reduce-scatter.19.cloned.1.call-done = f32[256,1024]{1,0:T(8,128)} async-done(((f32[1024,1024]{1,0:T(8,128)}), f32[256,1024]{1,0:T(8,128)}) %reduce-scatter.19.cloned.1.call-update) | async-done | bytes 1048592 | tf_op jit(solution)/shard_map/reduce_scatter | solution.py:94
  804.2 72.5 %reduce-scatter.15.cloned.1.call-done = f32[256,1024]{1,0:T(8,128)} async-done(((f32[1024,1024]{1,0:T(8,128)}), f32[256,1024]{1,0:T(8,128)}) %reduce-scatter.15.cloned.1.call-update) | async-done | bytes 1048592 | tf_op jit(solution)/shard_map/reduce_scatter | solution.py:85
  880.6 46.6 %all-gather.21.cloned.1.call-done = bf16[1024,1024]{1,0:T(8,128)(2,1)} async-done(((bf16[256,1024]{1,0:T(8,128)(2,1)}), bf16[1024,1024]{1,0:T(8,128)(2,1)}) %all-gather.21.cloned.1.call-update) | async-done | bytes 2097168 | tf_op jit(solution)/shard_map/all_gather | solution.py:65
  931.7 8.6 all-gather.23.cloned.1.call-start
  940.3 22.0 %reduce-scatter.21.cloned.1.call-done = f32[1024,256]{1,0:T(8,128)} async-done(((f32[1024,512]{1,0:T(8,128)}), f32[1024,256]{1,0:T(8,128)}) %reduce-scatter.21.cloned.1.call-update) | async-done | bytes 1048592 | tf_op jit(solution)/shard_map/reduce_scatter | solution.py:77
  966.5 61.6 %while.32 = (s32[]{:T(128)}, f32[1024,4,64]{0,2,1:T(8,128)}, f32[1024,4,64]{0,2,1:T(8,128)}, f32[2,512,4,64]{1,0,3,2:T(2,128)}, s32[2]{0:T(128)S(1)}, /*index=5*...) while((s32[]{:T(128)}, f32[1024,4,64]{0,2,1:T(8,128)}, ...), condition=%wide.region_25.26_spmd.clone, body=%wide.region_23.25_spmd.clone.sunk | while | flops 1375599104 | bytes 91288184 | solution.py:183
  986.3 10.4 dynamic_update_slice.28
  1017.6 10.4 dynamic_update_slice.28
  1049.1 7.3 fusion.39
  1056.4 11.2 convert_bitcast_fusion
  1069.9 24.0 %all-gather.23.cloned.1.call-done = bf16[1024,3,512]{2,0,1:T(8,128)(2,1)} async-done(((bf16[1024,3,256]{2,0,1:T(8,128)(2,1)}), bf16[1024,3,512]{2,0,1:T(8,128)(2,1)}) %all-gather.23.cloned.1.call-update) | async-done | bytes 3145744 | tf_op jit(solution)/shard_map/all_gather | solution.py:81
  1093.9 7.7 convert_bitcast_fusion.1
  1111.0 7.9 psum.130
  1119.4 208.6 %all-reduce.8.cloned.1.call-done = (bf16[1,1024,2,1408]{3,1,2,0:T(8,128)(2,1)}, bf16[1,1024,3,512]{3,1,2,0:T(8,128)(2,1)}, bf16[1,512,1024]{2,1,0:T(8,128)(2,1)}, bf16[1,1408,1024]{2,1,0:T(8,128)(2,1)}) async-done(((bf16[1,1024,2,1408]{3,1,2,0:T(8,128)(2,1)}, bf16[1,1024,3,512]{3,1,2,0:T(8,128)(2,1)}, bf16[1,512,1024]{2,1,0:T(8,128)(2,1)}, bf16[1,1408,1024]{2,1,0:T(8,128)(2,1)}), ...) | async-done | bytes 12845072 | tf_op jit(solution)/shard_map/psum | solution.py:363
  1330.8 12.8 copy.45
  1350.5 56.6 %reduce-scatter.23.cloned.1.call-done = f32[256,1024]{1,0:T(8,128)} async-done(((f32[1024,1024]{1,0:T(8,128)}), f32[256,1024]{1,0:T(8,128)}) %reduce-scatter.23.cloned.1.call-update) | async-done | bytes 1048592 | tf_op jit(solution)/shard_map/reduce_scatter | solution.py:94
  1413.9 59.9 %all-reduce = (f32[1,1024]{1,0:T(1,128)}, f32[1,1024]{1,0:T(1,128)}, f32[1,1024]{1,0:T(1,128)}, f32[1,1024]{1,0:T(1,128)}) all-reduce(f32[1,1024]{1,0:T(1,128)S(1)} %bitcast.186, f32[1,1024]{1,0:T(1,128)S(1)} %bitcast.187, f32[1,1024]{1,0:T(1,128)S(1)} %bitcast.184, ...), channel_id=1, replica_groups=mesh['dp'=4,'row'=2,'col'=4] {'dp','col'}, use_global_device_ids=true, to_apply=%region_32.33 | all-reduce | flops 4096 | bytes 32768 | tf_op jit(solution)/shard_map/psum | solution.py:366
  (203 shorter events, 184.7 us)
Async XLA Ops:
  7.2 58.0 %copy-start = (bf16[1,1024,3,512]{3,1,2,0:T(8,128)(2,1)S(1)}, bf16[1,1024,3,512]{3,1,2,0:T(8,128)(2,1)}, u32[]{:S(2)}) copy-start(bf16[1,1024,3,512]{3,1,2,0:T(8,128)(2,1)} %param.18) | copy-start | bytes 9437188
  7.2 58.0 %all-gather.9.cloned.1.call-start = ((), (), s32[]{:S(2)}) async-start(), calls=%async_computation.8 | async-start | bytes 2621440 | tf_op jit(solution)/shard_map/all_gather | solution.py:61
  17.2 130.7 %reduce-scatter.9.cloned.1.call-start = ((), (), s32[]{:S(2)}) async-start(), calls=%async_computation.9 | async-start | bytes 9437184 | tf_op jit(solution)/shard_map/reduce_scatter | solution.py:69
  72.0 133.5 %all-gather.11.cloned.1.call-start = ((), (), s32[]{:S(2)}) async-start(), calls=%async_computation.10 | async-start | bytes 1572864 | tf_op jit(solution)/shard_map/all_gather | solution.py:73
  73.6 85.7 %copy-start.13 = (f32[1024,8]{0,1:T(8,128)}, f32[1024,8]{0,1:T(8,128)S(1)}, u32[]{:S(2)}) copy-start(f32[1024,8]{0,1:T(8,128)S(1)} %get-tuple-element.389) | copy-start | bytes 98308
  184.0 103.3 %reduce-scatter.11.cloned.1.call-start = ((), (), s32[]{:S(2)}) async-start(), calls=%async_computation.11 | async-start | bytes 5242880 | tf_op jit(solution)/shard_map/reduce_scatter | solution.py:85
  210.4 84.3 %copy-start.15 = (f32[1,1024]{1,0:T(1,128)S(1)}, f32[1,1024]{1,0:T(1,128)}, u32[]{:S(2)}) copy-start(f32[1,1024]{1,0:T(1,128)} %param.21) | copy-start | bytes 12292
  210.4 84.3 %copy-start.22 = (f32[1,1024]{1,0:T(1,128)S(1)}, f32[1,1024]{1,0:T(1,128)}, u32[]{:S(2)}) copy-start(f32[1,1024]{1,0:T(1,128)} %param.22) | copy-start | bytes 12292
  210.4 124.9 %all-gather.17.cloned.1.call-start = ((), (), s32[]{:S(2)}) async-start(), calls=%async_computation.16 | async-start | bytes 2621440 | tf_op jit(solution)/shard_map/all_gather | solution.py:65
  211.0 170.9 %all-gather.13.cloned.1.call-start = ((), (), s32[]{:S(2)}) async-start(), calls=%async_computation.12 | async-start | bytes 2621440 | tf_op jit(solution)/shard_map/all_gather | solution.py:61
  297.0 157.9 %reduce-scatter.17.cloned.1.call-start = ((), (), s32[]{:S(2)}) async-start(), calls=%async_computation.17 | async-start | bytes 8650752 | tf_op jit(solution)/shard_map/reduce_scatter | solution.py:77
  343.4 247.6 %reduce-scatter.13.cloned.1.call-start = ((), (), s32[]{:S(2)}) async-start(), calls=%async_computation.13 | async-start | bytes 17301504 | tf_op jit(solution)/shard_map/reduce_scatter | solution.py:69
  393.8 279.0 %all-gather.19.cloned.1.call-start = ((), (), s32[]{:S(2)}) async-start(), calls=%async_computation.18 | async-start | bytes 8650752 | tf_op jit(solution)/shard_map/all_gather | solution.py:81
  598.2 118.7 %all-gather.15.cloned.1.call-start = ((), (), s32[]{:S(2)}) async-start(), calls=%async_computation.14 | async-start | bytes 4325376 | tf_op jit(solution)/shard_map/all_gather | solution.py:73
  598.8 197.9 %reduce-scatter.19.cloned.1.call-start = ((), (), s32[]{:S(2)}) async-start(), calls=%async_computation.19 | async-start | bytes 5242880 | tf_op jit(solution)/shard_map/reduce_scatter | solution.py:94
  684.4 192.3 %reduce-scatter.15.cloned.1.call-start = ((), (), s32[]{:S(2)}) async-start(), calls=%async_computation.15 | async-start | bytes 5242880 | tf_op jit(solution)/shard_map/reduce_scatter | solution.py:85
  725.1 202.1 %all-gather.21.cloned.1.call-start = ((), (), s32[]{:S(2)}) async-start(), calls=%async_computation.20 | async-start | bytes 2621440 | tf_op jit(solution)/shard_map/all_gather | solution.py:65
  880.6 81.8 %reduce-scatter.21.cloned.1.call-start = ((), (), s32[]{:S(2)}) async-start(), calls=%async_computation.21 | async-start | bytes 3145728 | tf_op jit(solution)/shard_map/reduce_scatter | solution.py:77
  931.7 162.2 %all-gather.23.cloned.1.call-start = ((), (), s32[]{:S(2)}) async-start(), calls=%async_computation.22 | async-start | bytes 4718592 | tf_op jit(solution)/shard_map/all_gather | solution.py:81
  972.6 3.5 copy-start.6
  1002.8 4.6 copy-start.6
  1048.8 279.2 %all-reduce.8.cloned.1.call-start = ((), (), s32[]{:S(2)}) async-start(), calls=%async_computation.24 | async-start | bytes 25690112 | tf_op jit(solution)/shard_map/psum | solution.py:363
  1049.1 7.4 copy-start.24
  1056.4 11.2 copy-start.10
  1056.4 11.2 copy-start.25
  1101.6 305.5 %reduce-scatter.23.cloned.1.call-start = ((), (), s32[]{:S(2)}) async-start(), calls=%async_computation.23 | async-start | bytes 5242880 | tf_op jit(solution)/shard_map/reduce_scatter | solution.py:94
  1330.8 12.8 copy-start.9
  1346.8 60.3 %copy-start.14 = (f32[1,1024]{1,0:T(1,128)S(1)}, f32[1,1024]{1,0:T(1,128)}, u32[]{:S(2)}) copy-start(f32[1,1024]{1,0:T(1,128)} %param.16) | copy-start | bytes 12292
  1346.8 60.3 %copy-start.19 = (f32[256]{0:T(256)S(1)}, f32[256]{0:T(256)}, u32[]{:S(2)}) copy-start(f32[256]{0:T(256)} %copy-done.18) | copy-start | bytes 3076
  1346.8 60.3 %copy-start.21 = (f32[256]{0:T(256)S(1)}, f32[256]{0:T(256)}, u32[]{:S(2)}) copy-start(f32[256]{0:T(256)} %copy-done.20) | copy-start | bytes 3076
  1346.8 67.1 %copy-start.16 = (f32[1024]{0:T(1024)S(1)}, f32[1024]{0:T(1024)}, u32[]{:S(2)}) copy-start(f32[1024]{0:T(1024)} %get-tuple-element.300) | copy-start | bytes 12292
  1346.8 67.1 %copy-start.17 = (f32[1024]{0:T(1024)S(1)}, f32[1024]{0:T(1024)}, u32[]{:S(2)}) copy-start(f32[1024]{0:T(1024)} %get-tuple-element.306) | copy-start | bytes 12292
  (20 other events, 33.4 us)
Sparse Core Ops, SparseCore 0:
  17.4 47.7 all-gather.8
  72.2 75.7 reduce-scatter.8
  184.2 21.3 all-gather.10
  210.5 76.7 reduce-scatter.10
  288.7 46.4 all-gather.16
  337.2 44.6 all-gather.12
  384.8 70.0 reduce-scatter.16
  457.9 133.1 reduce-scatter.12
  598.3 74.4 all-gather.18
  674.9 41.9 all-gather.14
  719.9 76.7 reduce-scatter.18
  799.4 77.2 reduce-scatter.14
  880.7 46.4 all-gather.20
  931.8 30.5 reduce-scatter.20
  1048.9 44.9 all-gather.22
  1101.7 226.2 all-reduce.7
  1330.1 76.9 reduce-scatter.22
where the time goes:
time: 1490 us; the launch traced here: 1480 us
  waiting for transfers between devices  1100 us (74%)
  matrix products  127 us (9%)
  blocking collectives  88.4 us (6%)
  other arithmetic  67.5 us (5%)
  local copies, waits for them, and re-layouts  66.9 us (4%)
    reduce_scatter x2, waiting for transfers between devices, split_units(): return lax.psum_scatter(partial_sum, 'row', scatter_dimension=2, tiled=True)  211 us
    psum x1, waiting for transfers between devices, local(): lax.psum(stack_gate.astype(jnp.bfloat16), 'dp').astype(jnp.float32)  209 us
    reduce_scatter x2, waiting for transfers between devices, branch_sum(): lax.psum_scatter(jnp.dot(full_rows, weight_block, preferred_element_type=...  149 us
    reduce_scatter x2, waiting for transfers between devices, input_sum(): lax.psum_scatter(jnp.einsum('stk,dtk->sd', grad_full, weight_block, prefe...  128 us
    all_gather x2, waiting for transfers between devices, join_unit_grads(): return lax.all_gather(local_units, 'row', axis=2, tiled=True)  98 us
    all_gather x2, waiting for transfers between devices, gather_tokens(): return lax.all_gather(local_low, 'col', axis=0, tiled=True)  86.3 us
    all_gather x2, waiting for transfers between devices, gather_gradient(): return lax.all_gather(local_low, 'col', axis=0, tiled=True)  84.5 us
    reduce_scatter x2, waiting for transfers between devices, split_unit_grads(): return lax.psum_scatter(partial_sum, 'row', scatter_dimension=1, tiled=True)  83 us
  transfers between devices with their start and end apart: 17, of which 17 were waited for; matrix products, arithmetic and copies ran while one was open for 7% of the time, Pallas kernels for 0%

commit v1 on v0

--- a/solution.py
+++ b/solution.py
@@ -8,6 +8,19 @@
 ROT = 16
 LENGTH = 1024
 EPSILON = 1e-05
+
+
+def gather_around(value, axis, dim):
+    ways = lax.axis_size(axis)
+    up = [(d, (d + 1) % ways) for d in range(ways)]
+    down = [(d, (d - 1) % ways) for d in range(ways)]
+    earlier, later = ([value], [value])
+    for _ in range(ways // 2):
+        earlier.append(lax.ppermute(earlier[-1], axis, up))
+    for _ in range((ways - 1) // 2):
+        later.append(lax.ppermute(later[-1], axis, down))
+    line = jnp.concatenate([*earlier[::-1], *later[1:]], axis=dim)
+    return jnp.roll(line, (lax.axis_index(axis) - ways // 2) * value.shape[dim], axis=dim)
 
 
 def rotary_tables(tokens):
@@ -58,7 +71,7 @@
 
 
 def gather_tokens(local_low):
-    return lax.all_gather(local_low, "col", axis=0, tiled=True)
+    return gather_around(local_low, "col", 0)
 
 
 def gather_gradient(local_low):

time: 1490 us -> 1450 us (0.973)
  waiting for transfers between devices: 1100 us -> 1030 us
    all_gather x2, waiting for transfers between devices: 86.3 us -> 0.01 us  [weight_product(): lax.all_gather(local_low, 'col', axis=0, tiled=True)]
    ppermute x0 -> x6, waiting for transfers between devices: none -> 52.5 us  [the longest x4 46.2 us: gather_around(): earlier.append(lax.ppermute(earlier[-1], axis, up))]
    reduce_scatter x2, waiting for transfers between devices: 83 us -> 41 us  [split_unit_grads(): return lax.psum_scatter(partial_sum, 'row', scatter_dimension=1, tiled=True)]
    ppermute x0 -> x6, starting transfers between devices: none -> 22.3 us  [the longest x4 17.9 us: gather_around(): earlier.append(lax.ppermute(earlier[-1], axis, up))]
  transfers between devices with their start and end apart: 17 -> 23, of which waited for: 17 -> 21; matrix products, arithmetic and copies ran while one was open for 7% -> 13% of each run, Pallas kernels for 0% -> 0%
where the time goes in v1:
time: 1450 us; the launch traced here: 1440 us
  waiting for transfers between devices  1030 us (71%)
  matrix products  134 us (9%)
  blocking collectives  88.4 us (6%)
  other arithmetic  67.5 us (5%)
  local copies, waits for them, and re-layouts  66.9 us (5%)
  starting transfers between devices  24 us (2%)
  between operations  14.6 us (1%)
    reduce_scatter x2, waiting for transfers between devices, split_units(): return lax.psum_scatter(partial_sum, 'row', scatter_dimension=2, tiled=True)  211 us
    psum x1, waiting for transfers between devices, local(): lax.psum(stack_gate.astype(jnp.bfloat16), 'dp').astype(jnp.float32)  209 us
    reduce_scatter x2, waiting for transfers between devices, branch_sum(): lax.psum_scatter(jnp.dot(full_rows, weight_block, preferred_element_type=...  142 us
    reduce_scatter x2, waiting for transfers between devices, input_sum(): lax.psum_scatter(jnp.einsum('stk,dtk->sd', grad_full, weight_block, prefe...  128 us
    all_gather x2, waiting for transfers between devices, join_unit_grads(): return lax.all_gather(local_units, 'row', axis=2, tiled=True)  105 us
    all_gather x2, waiting for transfers between devices, gather_gradient(): return lax.all_gather(local_low, 'col', axis=0, tiled=True)  89.3 us
    psum x1, blocking collectives, local(): lax.psum((jnp.stack(gain_a_grads), jnp.stack(shift_a_grads), jnp.stack(ga...  59.9 us
    all_gather x2, waiting for transfers between devices, join_units(): return lax.all_gather(local_units, 'row', axis=1, tiled=True)  53.1 us
  transfers between devices with their start and end apart: 23, of which 21 were waited for; matrix products, arithmetic and copies ran while one was open for 13% of the time, Pallas kernels for 0%

profile of v1, /device:TPU:0, one launch (start us, length us, event | category | flops | bytes accessed | tf_op | source)
XLA Modules:
  0.0 1436.4 jit_solution(10117988568369983005)
XLA Ops:
  21.4 13.2 collective-permute-done
  44.6 10.4 collective-permute-done.1
  55.0 9.9 fusion.42
  66.4 75.1 %reduce-scatter.9.cloned.1.call-done = f32[1024,3,256]{2,0,1:T(8,128)} async-done(((f32[1024,3,512]{2,0,1:T(8,128)}), f32[1024,3,256]{2,0,1:T(8,128)}) %reduce-scatter.9.cloned.1.call-update) | async-done | bytes 3145744 | tf_op jit(solution)/shard_map/reduce_scatter | solution.py:82
  153.9 21.1 %while.31 = (s32[]{:T(128)}, bf16[2,512,4,64]{1,3,2,0:T(8,128)(2,1)}, f32[2,4,512]{2,1,0:T(4,128)S(1)}, s32[2]{0:T(128)S(1)}, bf16[1024,4,64]{0,2,1:T(8,128)(2,1...) while((s32[]{:T(128)}, ...), condition=%wide.region_8.10_spmd, body=%wide.region_5.9_spmd.sunk | while | flops 562559488 | bytes 35459536 | solution.py:157
  178.5 20.5 %all-gather.9.cloned.1.call-done = bf16[1024,512]{0,1:T(8,128)(2,1)} async-done(((bf16[1024,256]{0,1:T(8,128)(2,1)}), bf16[1024,512]{0,1:T(8,128)(2,1)}) %all-gather.9.cloned.1.call-update) | async-done | bytes 1048592 | tf_op jit(solution)/shard_map/all_gather | solution.py:86
  203.9 42.7 %all-gather.13.cloned.1.call-done = bf16[1024,1024]{1,0:T(8,128)(2,1)} async-done(((bf16[256,1024]{1,0:T(8,128)(2,1)}), bf16[1024,1024]{1,0:T(8,128)(2,1)}) %all-gather.13.cloned.1.call-update) | async-done | bytes 2097168 | tf_op jit(solution)/shard_map/all_gather | solution.py:78
  246.6 8.3 fusion.44
  255.0 69.9 %reduce-scatter.11.cloned.1.call-done = f32[256,1024]{1,0:T(8,128)} async-done(((f32[1024,1024]{1,0:T(8,128)}), f32[256,1024]{1,0:T(8,128)}) %reduce-scatter.11.cloned.1.call-update) | async-done | bytes 1048592 | tf_op jit(solution)/shard_map/reduce_scatter | solution.py:98
  338.4 13.1 collective-permute-done.3
  362.1 9.6 collective-permute-done.4
  371.7 15.9 %fusion.35 = f32[1024,2,1408]{0,2,1:T(8,128)} fusion(bf16[1024,2,1408]{2,1,0:T(2,128)(2,1)} %bitcast.191, s32[]{:T(128)S(6)} %select_n.107, bf16[256,1024]{1,0:T(8,128)(2,1)S(1)} %collective-permute-done.4, bf16[256,1024]{1,0:T(8,128)(2,1)S(1)} %collective-permute-done.3, bf16[256,1024]{1,0:T(8,128)(2,1)} %add_convert_fusion.1, ...), kind=kOutput, calls=%fused_computation.45 | convolution fusion | flops 5922357248 | bytes 19398660 | tf_op jit(solution)/shard_map/sd,dtf->stf/dot_general | solution.py:246
  387.7 11.9 reduce-scatter.17.cloned.1.call-done
  399.5 136.0 %reduce-scatter.13.cloned.1.call-done = f32[1024,2,704]{0,2,1:T(8,128)} async-done(((f32[1024,2,1408]{0,2,1:T(8,128)}), f32[1024,2,704]{0,2,1:T(8,128)}) %reduce-scatter.13.cloned.1.call-update) | async-done | bytes 5767184 | tf_op jit(solution)/shard_map/reduce_scatter | solution.py:82
  543.9 73.4 %all-gather.15.cloned.1.call-done = bf16[1024,2,1408]{0,2,1:T(8,128)(2,1)} async-done(((bf16[1024,2,704]{0,2,1:T(8,128)(2,1)}), bf16[1024,2,1408]{0,2,1:T(8,128)(2,1)}) %all-gather.15.cloned.1.call-update) | async-done | bytes 5767184 | tf_op jit(solution)/shard_map/all_gather | solution.py:94
  617.4 11.5 fusion.51
  628.9 32.7 %all-gather.11.cloned.1.call-done = bf16[1024,1408]{0,1:T(8,128)(2,1)} async-done(((bf16[1024,704]{0,1:T(8,128)(2,1)}), bf16[1024,1408]{0,1:T(8,128)(2,1)}) %all-gather.11.cloned.1.call-update) | async-done | bytes 2883600 | tf_op jit(solution)/shard_map/all_gather | solution.py:86
  661.6 8.2 fusion.46
  669.8 71.5 %reduce-scatter.19.cloned.1.call-done = f32[256,1024]{1,0:T(8,128)} async-done(((f32[1024,1024]{1,0:T(8,128)}), f32[256,1024]{1,0:T(8,128)}) %reduce-scatter.19.cloned.1.call-update) | async-done | bytes 1048592 | tf_op jit(solution)/shard_map/reduce_scatter | solution.py:107
  748.9 72.5 %reduce-scatter.15.cloned.1.call-done = f32[256,1024]{1,0:T(8,128)} async-done(((f32[1024,1024]{1,0:T(8,128)}), f32[256,1024]{1,0:T(8,128)}) %reduce-scatter.15.cloned.1.call-update) | async-done | bytes 1048592 | tf_op jit(solution)/shard_map/reduce_scatter | solution.py:98
  825.3 46.5 %all-gather.17.cloned.1.call-done = bf16[1024,1024]{1,0:T(8,128)(2,1)} async-done(((bf16[256,1024]{1,0:T(8,128)(2,1)}), bf16[1024,1024]{1,0:T(8,128)(2,1)}) %all-gather.17.cloned.1.call-update) | async-done | bytes 2097168 | tf_op jit(solution)/shard_map/all_gather | solution.py:78
  877.9 29.1 %reduce-scatter.21.cloned.1.call-done = f32[1024,256]{1,0:T(8,128)} async-done(((f32[1024,512]{1,0:T(8,128)}), f32[1024,256]{1,0:T(8,128)}) %reduce-scatter.21.cloned.1.call-update) | async-done | bytes 1048592 | tf_op jit(solution)/shard_map/reduce_scatter | solution.py:90
  911.1 61.6 %while.32 = (s32[]{:T(128)}, f32[1024,4,64]{0,2,1:T(8,128)}, f32[1024,4,64]{0,2,1:T(8,128)}, f32[2,512,4,64]{1,0,3,2:T(2,128)}, s32[2]{0:T(128)S(1)}, /*index=5*...) while((s32[]{:T(128)}, f32[1024,4,64]{0,2,1:T(8,128)}, ...), condition=%wide.region_25.27_spmd.clone, body=%wide.region_23.26_spmd.clone.sunk | while | flops 1375599104 | bytes 91288184 | solution.py:196
  931.0 10.4 dynamic_update_slice.28
  962.4 10.4 dynamic_update_slice.28
  1001.0 11.1 convert_bitcast_fusion
  1014.4 31.9 %all-gather.19.cloned.1.call-done = bf16[1024,3,512]{2,0,1:T(8,128)(2,1)} async-done(((bf16[1024,3,256]{2,0,1:T(8,128)(2,1)}), bf16[1024,3,512]{2,0,1:T(8,128)(2,1)}) %all-gather.19.cloned.1.call-update) | async-done | bytes 3145744 | tf_op jit(solution)/shard_map/all_gather | solution.py:94
  1063.4 7.9 psum.130
  1071.9 208.6 %all-reduce.8.cloned.1.call-done = (bf16[1,1024,2,1408]{3,1,2,0:T(8,128)(2,1)}, bf16[1,1024,3,512]{3,1,2,0:T(8,128)(2,1)}, bf16[1,512,1024]{2,1,0:T(8,128)(2,1)}, bf16[1,1408,1024]{2,1,0:T(8,128)(2,1)}) async-done(((bf16[1,1024,2,1408]{3,1,2,0:T(8,128)(2,1)}, bf16[1,1024,3,512]{3,1,2,0:T(8,128)(2,1)}, bf16[1,512,1024]{2,1,0:T(8,128)(2,1)}, bf16[1,1408,1024]{2,1,0:T(8,128)(2,1)}), ...) | async-done | bytes 12845072 | tf_op jit(solution)/shard_map/psum | solution.py:376
  1283.2 12.8 copy.45
  1302.9 56.6 %reduce-scatter.23.cloned.1.call-done = f32[256,1024]{1,0:T(8,128)} async-done(((f32[1024,1024]{1,0:T(8,128)}), f32[256,1024]{1,0:T(8,128)}) %reduce-scatter.23.cloned.1.call-update) | async-done | bytes 1048592 | tf_op jit(solution)/shard_map/reduce_scatter | solution.py:107
  1366.4 59.9 %all-reduce = (f32[1,1024]{1,0:T(1,128)}, f32[1,1024]{1,0:T(1,128)}, f32[1,1024]{1,0:T(1,128)}, f32[1,1024]{1,0:T(1,128)}) all-reduce(f32[1,1024]{1,0:T(1,128)S(1)} %bitcast.186, f32[1,1024]{1,0:T(1,128)S(1)} %bitcast.187, f32[1,1024]{1,0:T(1,128)S(1)} %bitcast.184, ...), channel_id=1, replica_groups=mesh['dp'=4,'row'=2,'col'=4] {'dp','col'}, use_global_device_ids=true, to_apply=%region_32.34 | all-reduce | flops 4096 | bytes 32768 | tf_op jit(solution)/shard_map/psum | solution.py:379
  (213 shorter events, 223.3 us)
Async XLA Ops:
  7.2 47.8 %copy-start = (bf16[1,1024,3,512]{3,1,2,0:T(8,128)(2,1)S(1)}, bf16[1,1024,3,512]{3,1,2,0:T(8,128)(2,1)}, u32[]{:S(2)}) copy-start(bf16[1,1024,3,512]{3,1,2,0:T(8,128)(2,1)} %param.20) | copy-start | bytes 9437188
  7.2 134.3 %reduce-scatter.9.cloned.1.call-start = ((), (), s32[]{:S(2)}) async-start(), calls=%async_computation.8 | async-start | bytes 9437184 | tf_op jit(solution)/shard_map/reduce_scatter | solution.py:82
  17.2 17.3 %collective-permute-start = (bf16[256,1024]{1,0:T(8,128)(2,1)}, bf16[256,1024]{1,0:T(8,128)(2,1)}, u32[]{:S(2)}, u32[]{:S(2)}) collective-permute-start(bf16[256,1024]{1,0:T(8,128)(2,1)} %fusion.85), channel_id=1, source_target_pairs={{0,1},{1,2},{2,3},{3,0},{4,5},{5,6},{6,7},{7,4},{8,9},{9,10},{10,1... | collective-permute-start | bytes 1572872 | tf_op jit(solution)/shard_map/ppermute | solution.py:19
  19.3 25.2 %collective-permute-start.2 = (bf16[256,1024]{1,0:T(8,128)(2,1)}, bf16[256,1024]{1,0:T(8,128)(2,1)}, u32[]{:S(2)}, u32[]{:S(2)}) collective-permute-start(bf16[256,1024]{1,0:T(8,128)(2,1)} %fusion.85), channel_id=1, source_target_pairs={{0,3},{1,0},{2,1},{3,2},{4,7},{5,4},{6,5},{7,6},{8,11},{9,8},{10,9... | collective-permute-start | bytes 1572872 | tf_op jit(solution)/shard_map/ppermute | solution.py:21
  34.6 20.4 %collective-permute-start.1 = (bf16[256,1024]{1,0:T(8,128)(2,1)}, bf16[256,1024]{1,0:T(8,128)(2,1)}, u32[]{:S(2)}, u32[]{:S(2)}) collective-permute-start(bf16[256,1024]{1,0:T(8,128)(2,1)} %collective-permute-done), channel_id=1, source_target_pairs={{0,1},{1,2},{2,3},{3,0},{4,5},{5,6},{6,7},{7,4},{8,9},{9,10},{10,1... | collective-permute-start | bytes 1572872 | tf_op jit(solution)/shard_map/ppermute | solution.py:19
  64.9 134.1 %all-gather.9.cloned.1.call-start = ((), (), s32[]{:S(2)}) async-start(), calls=%async_computation.9 | async-start | bytes 1572864 | tf_op jit(solution)/shard_map/all_gather | solution.py:86
  66.4 86.3 %copy-start.13 = (f32[1024,8]{0,1:T(8,128)}, f32[1024,8]{0,1:T(8,128)S(1)}, u32[]{:S(2)}) copy-start(f32[1024,8]{0,1:T(8,128)S(1)} %get-tuple-element.390) | copy-start | bytes 98308
  177.5 69.1 %all-gather.13.cloned.1.call-start = ((), (), s32[]{:S(2)}) async-start(), calls=%async_computation.14 | async-start | bytes 2621440 | tf_op jit(solution)/shard_map/all_gather | solution.py:78
  178.2 146.7 %reduce-scatter.11.cloned.1.call-start = ((), (), s32[]{:S(2)}) async-start(), calls=%async_computation.10 | async-start | bytes 5242880 | tf_op jit(solution)/shard_map/reduce_scatter | solution.py:98
  203.8 195.7 %reduce-scatter.17.cloned.1.call-start = ((), (), s32[]{:S(2)}) async-start(), calls=%async_computation.15 | async-start | bytes 8650752 | tf_op jit(solution)/shard_map/reduce_scatter | solution.py:90
  254.9 77.4 %copy-start.15 = (f32[1,1024]{1,0:T(1,128)S(1)}, f32[1,1024]{1,0:T(1,128)}, u32[]{:S(2)}) copy-start(f32[1,1024]{1,0:T(1,128)} %param.23) | copy-start | bytes 12292
  254.9 77.4 %copy-start.22 = (f32[1,1024]{1,0:T(1,128)S(1)}, f32[1,1024]{1,0:T(1,128)}, u32[]{:S(2)}) copy-start(f32[1,1024]{1,0:T(1,128)} %param.24) | copy-start | bytes 12292
  255.0 280.6 %reduce-scatter.13.cloned.1.call-start = ((), (), s32[]{:S(2)}) async-start(), calls=%async_computation.11 | async-start | bytes 17301504 | tf_op jit(solution)/shard_map/reduce_scatter | solution.py:82
  334.6 16.9 %collective-permute-start.3 = (bf16[256,1024]{1,0:T(8,128)(2,1)}, bf16[256,1024]{1,0:T(8,128)(2,1)S(1)}, u32[]{:S(2)}, u32[]{:S(2)}) collective-permute-start(bf16[256,1024]{1,0:T(8,128)(2,1)} %add_convert_fusion.1), channel_id=1, source_target_pairs={{0,1},{1,2},{2,3},{3,0},{4,5},{5,6},{6,7},{7,4},{8,9},{9,10},{10,1... | collective-permute-start | bytes 1572872 | tf_op jit(solution)/shard_map/ppermute | solution.py:19
  336.1 26.0 %collective-permute-start.5 = (bf16[256,1024]{1,0:T(8,128)(2,1)}, bf16[256,1024]{1,0:T(8,128)(2,1)S(1)}, u32[]{:S(2)}, u32[]{:S(2)}) collective-permute-start(bf16[256,1024]{1,0:T(8,128)(2,1)} %add_convert_fusion.1), channel_id=1, source_target_pairs={{0,3},{1,0},{2,1},{3,2},{4,7},{5,4},{6,5},{7,6},{8,11},{9,8},{10,9... | collective-permute-start | bytes 1572872 | tf_op jit(solution)/shard_map/ppermute | solution.py:21
  351.5 20.2 %collective-permute-start.4 = (bf16[256,1024]{1,0:T(8,128)(2,1)S(1)}, bf16[256,1024]{1,0:T(8,128)(2,1)S(1)}, u32[]{:S(2)}, u32[]{:S(2)}) collective-permute-start(bf16[256,1024]{1,0:T(8,128)(2,1)S(1)} %collective-permute-done.3), channel_id=1, source_target_pairs={{0,1},{1,2},{2,3},{3,0},{4,5},{5,6},{6,7},{7,4},{8,9},{9,10},{10,1... | collective-permute-start | bytes 1572872 | tf_op jit(solution)/shard_map/ppermute | solution.py:19
  387.6 229.7 %all-gather.15.cloned.1.call-start = ((), (), s32[]{:S(2)}) async-start(), calls=%async_computation.16 | async-start | bytes 8650752 | tf_op jit(solution)/shard_map/all_gather | solution.py:94
  542.7 118.9 %all-gather.11.cloned.1.call-start = ((), (), s32[]{:S(2)}) async-start(), calls=%async_computation.12 | async-start | bytes 4325376 | tf_op jit(solution)/shard_map/all_gather | solution.py:86
  543.5 197.9 %reduce-scatter.19.cloned.1.call-start = ((), (), s32[]{:S(2)}) async-start(), calls=%async_computation.17 | async-start | bytes 5242880 | tf_op jit(solution)/shard_map/reduce_scatter | solution.py:107
  628.9 192.5 %reduce-scatter.15.cloned.1.call-start = ((), (), s32[]{:S(2)}) async-start(), calls=%async_computation.13 | async-start | bytes 5242880 | tf_op jit(solution)/shard_map/reduce_scatter | solution.py:98
  669.8 202.1 %all-gather.17.cloned.1.call-start = ((), (), s32[]{:S(2)}) async-start(), calls=%async_computation.18 | async-start | bytes 2621440 | tf_op jit(solution)/shard_map/all_gather | solution.py:78
  825.3 81.8 %reduce-scatter.21.cloned.1.call-start = ((), (), s32[]{:S(2)}) async-start(), calls=%async_computation.19 | async-start | bytes 3145728 | tf_op jit(solution)/shard_map/reduce_scatter | solution.py:90
  876.4 124.7 %all-gather.23.cloned.1.call-start = ((), (), s32[]{:S(2)}) async-start(), calls=%async_computation.23 | async-start | bytes 2621440 | tf_op jit(solution)/shard_map/all_gather | solution.py:119
  877.1 137.3 %all-gather.21.cloned.1.call-start = ((), (), s32[]{:S(2)}) async-start(), calls=%async_computation.22 | async-start | bytes 2621440 | tf_op jit(solution)/shard_map/all_gather | solution.py:119
  877.7 168.6 %all-gather.19.cloned.1.call-start = ((), (), s32[]{:S(2)}) async-start(), calls=%async_computation.20 | async-start | bytes 4718592 | tf_op jit(solution)/shard_map/all_gather | solution.py:94
  993.6 286.9 %all-reduce.8.cloned.1.call-start = ((), (), s32[]{:S(2)}) async-start(), calls=%async_computation.24 | async-start | bytes 25690112 | tf_op jit(solution)/shard_map/psum | solution.py:376
  1054.0 305.5 %reduce-scatter.23.cloned.1.call-start = ((), (), s32[]{:S(2)}) async-start(), calls=%async_computation.21 | async-start | bytes 5242880 | tf_op jit(solution)/shard_map/reduce_scatter | solution.py:107
  1299.3 60.3 %copy-start.14 = (f32[1,1024]{1,0:T(1,128)S(1)}, f32[1,1024]{1,0:T(1,128)}, u32[]{:S(2)}) copy-start(f32[1,1024]{1,0:T(1,128)} %param.18) | copy-start | bytes 12292
  1299.3 60.3 %copy-start.19 = (f32[256]{0:T(256)S(1)}, f32[256]{0:T(256)}, u32[]{:S(2)}) copy-start(f32[256]{0:T(256)} %copy-done.18) | copy-start | bytes 3076
  1299.3 60.3 %copy-start.21 = (f32[256]{0:T(256)S(1)}, f32[256]{0:T(256)}, u32[]{:S(2)}) copy-start(f32[256]{0:T(256)} %copy-done.20) | copy-start | bytes 3076
  1299.3 67.1 %copy-start.16 = (f32[1024]{0:T(1024)S(1)}, f32[1024]{0:T(1024)}, u32[]{:S(2)}) copy-start(f32[1024]{0:T(1024)} %get-tuple-element.301) | copy-start | bytes 12292
  1299.3 67.1 %copy-start.17 = (f32[1024]{0:T(1024)S(1)}, f32[1024]{0:T(1024)}, u32[]{:S(2)}) copy-start(f32[1024]{0:T(1024)} %get-tuple-element.307) | copy-start | bytes 12292
  (25 other events, 76.6 us)
Sparse Core Ops, SparseCore 0:
  65.0 76.3 reduce-scatter.8
  177.6 21.2 all-gather.8
  200.6 45.9 all-gather.12
  249.4 75.4 reduce-scatter.10
  327.7 71.8 reduce-scatter.16
  402.4 133.1 reduce-scatter.12
  542.9 74.4 all-gather.14
  619.6 41.9 all-gather.10
  664.6 76.7 reduce-scatter.18
  744.1 77.2 reduce-scatter.14
  825.4 46.4 all-gather.16
  876.5 30.5 reduce-scatter.20
  908.6 45.9 all-gather.22
  956.0 44.6 all-gather.20
  1002.7 43.6 all-gather.18
  1054.1 226.2 all-reduce.7
  1282.6 76.9 reduce-scatter.22
